TPU v7x, 256 devices: a whole 4x4x8 slice. The times are simulated.
256 devices in a mesh: col: 4 (over z_lo, core), dp: 64 (over y, x, z_hi).
Axes of the slice: x: 4, y: 4, z: 8 (z_hi: 4, z_lo: 2; z = z_hi * 2 + z_lo), core: 2. Of those that a mesh axis runs over, the one named last changes fastest.
Arguments:
- layer_input: bfloat16 [8192, 8192], P('dp', 'col'), may hold values from -6 to 6
- query_cotangent: bfloat16 [8192, 4096], P('dp'), may hold values from -0.06591797 to 0.06591797
- key_cotangent: bfloat16 [8192, 1024], P('dp'), may hold values from -0.06591797 to 0.06591797
- up_cotangent: bfloat16 [8192, 14336], P('dp'), may hold values from -0.06591797 to 0.06591797
- query_weight: bfloat16 [4096, 8192], P('dp', 'col'), may hold values from -24 to 24
- key_weight: bfloat16 [1024, 8192], P('dp', 'col'), may hold values from -24 to 24
- up_weight: bfloat16 [14336, 8192], P('dp', 'col'), may hold values from -24 to 24
- moment_query: bfloat16 [4096, 8192], P('dp', 'col'), may hold values from -3 to 3
- moment_key: bfloat16 [1024, 8192], P('dp', 'col'), may hold values from -3 to 3
- moment_up: bfloat16 [14336, 8192], P('dp', 'col'), may hold values from -3 to 3
- second_query: bfloat16 [4096, 8192], P('dp', 'col'), may hold values from 0.25 to 4
- second_key: bfloat16 [1024, 8192], P('dp', 'col'), may hold values from 0.25 to 4
- second_up: bfloat16 [14336, 8192], P('dp', 'col'), may hold values from 0.25 to 4
Outputs:
- updated_query: bfloat16 [4096, 8192], P('dp', 'col')
- updated_key: bfloat16 [1024, 8192], P('dp', 'col')
- updated_up: bfloat16 [14336, 8192], P('dp', 'col')
- mean_query: bfloat16 [4096, 8192], P('dp', 'col')
- mean_key: bfloat16 [1024, 8192], P('dp', 'col')
- mean_up: bfloat16 [14336, 8192], P('dp', 'col')
- square_query: bfloat16 [4096, 8192], P('dp', 'col')
- square_key: bfloat16 [1024, 8192], P('dp', 'col')
- square_up: bfloat16 [14336, 8192], P('dp', 'col')
All inputs are finite; a program needn't handle non-finite values.
Results may differ from a plain program's by a relative error of at most 0.001.
Values may be sent and summed in bfloat16 or wider, within the bound.
A program may use at most 128 MiB of HBM per device.

v0:
```python
import jax
import jax.numpy as jnp
from jax import lax
from jax.sharding import PartitionSpec as P

beta_one = 0.9
beta_two = 0.95
rate = 0.1
eps_adam = 1e-08
eps_norm = 1e-06


def contract_tokens(cotangent_rows, inputs):
    return lax.dot_general(
        cotangent_rows, inputs, (((0,), (0,)), ((), ())), preferred_element_type=jnp.float32
    )


def optimizer_pass(gradient, weight, moment, second):
    first = beta_one * moment.astype(jnp.float32) + (1.0 - beta_one) * gradient
    square = beta_two * second.astype(jnp.float32) + (1.0 - beta_two) * gradient * gradient
    step = weight.astype(jnp.float32) - rate * first / (jnp.sqrt(square) + eps_adam)
    partial_power = jnp.sum(step * step, axis=1)
    return (step, first.astype(jnp.bfloat16), square.astype(jnp.bfloat16), partial_power)


def finish_rows(step, total_power, width):
    scale = jnp.sqrt(total_power / width + eps_norm)
    return (step / scale[:, None]).astype(jnp.bfloat16)


def per_device(
    layer_input,
    query_cotangent,
    key_cotangent,
    up_cotangent,
    query_weight,
    key_weight,
    up_weight,
    moment_query,
    moment_key,
    moment_up,
    second_query,
    second_key,
    second_up,
):
    groups = lax.axis_size("dp")
    tok_local = layer_input.shape[0]
    query_rows = query_weight.shape[0]
    key_rows = key_weight.shape[0]
    up_rows = up_weight.shape[0]
    all_rows = query_rows + key_rows + up_rows
    width = layer_input.shape[1] * lax.axis_size("col")
    joined = jnp.concatenate(
        [
            query_cotangent.reshape(tok_local, groups, query_rows),
            key_cotangent.reshape(tok_local, groups, key_rows),
            up_cotangent.reshape(tok_local, groups, up_rows),
        ],
        axis=2,
    )
    owned = lax.all_to_all(joined, "dp", split_axis=1, concat_axis=0, tiled=True).reshape(
        -1, all_rows
    )
    gathered = lax.all_gather(layer_input, "dp", axis=0, tiled=True)
    gradient = contract_tokens(owned, gathered)
    grad_query = gradient[:query_rows]
    grad_key = gradient[query_rows : query_rows + key_rows]
    grad_up = gradient[query_rows + key_rows :]
    step_query, first_query, sq_query, power_query = optimizer_pass(
        grad_query, query_weight, moment_query, second_query
    )
    step_key, first_key, sq_key, power_key = optimizer_pass(
        grad_key, key_weight, moment_key, second_key
    )
    step_up, first_up, sq_up, power_up = optimizer_pass(grad_up, up_weight, moment_up, second_up)
    total_query, total_key, total_up = lax.psum((power_query, power_key, power_up), "col")
    new_query = finish_rows(step_query, total_query, width)
    new_key = finish_rows(step_key, total_key, width)
    new_up = finish_rows(step_up, total_up, width)
    return (new_query, new_key, new_up, first_query, first_key, first_up, sq_query, sq_key, sq_up)


def solution(mesh):
    placed = (
        P("dp", "col"),
        P("dp", None),
        P("dp", None),
        P("dp", None),
        P("dp", "col"),
        P("dp", "col"),
        P("dp", "col"),
        P("dp", "col"),
        P("dp", "col"),
        P("dp", "col"),
        P("dp", "col"),
        P("dp", "col"),
        P("dp", "col"),
    )
    return jax.shard_map(
        per_device,
        mesh=mesh,
        in_specs=placed,
        out_specs=(
            P("dp", "col"),
            P("dp", "col"),
            P("dp", "col"),
            P("dp", "col"),
            P("dp", "col"),
            P("dp", "col"),
            P("dp", "col"),
            P("dp", "col"),
            P("dp", "col"),
        ),
        check_vma=False,
    )
```

profile of v0, /device:TPU:6, one launch (start us, length us, event | category | flops | bytes accessed | tf_op | source)
XLA Modules:
  0.0 440.0 jit_solution(7235209890121948709)
XLA Ops:
  7.2 0.0 all-gather.2.cloned.1.call-start
  7.2 0.7 all-gather.2.cloned.1.call-update
  7.9 6.1 %copy.24 = bf16[128,14336]{0,1:T(8,128)(2,1)} copy(bf16[128,14336]{1,0:T(8,128)(2,1)} %param.16) | data formatting | bytes 7340032 | tf_op args[3]
  14.1 0.7 copy.22
  14.7 0.2 copy.23
  14.9 2.2 pad_maximum_fusion
  17.2 182.4 %all_to_all.15 = bf16[128,64,304]{0,2,1:T(8,128)(2,1)S(1)} all-to-all(bf16[128,64,304]{0,2,1:T(8,128)(2,1)S(1)} %pad_maximum_fusion), channel_id=1, replica_groups=mesh['col'=4,'dp'=64] {'dp'}, dimensions={1} | all-to-all | bytes 9961472 | tf_op jit(solution)/shard_map/all_to_all | solution.py:62
  199.6 3.6 copy.25
  203.2 188.7 %all-gather.2.cloned.1.call-done = bf16[8192,2048]{1,0:T(8,128)(2,1)} async-done(((bf16[128,2048]{1,0:T(8,128)(2,1)}), bf16[8192,2048]{1,0:T(8,128)(2,1)}) %all-gather.2.cloned.1.call-update) | async-done | bytes 33554448 | tf_op jit(solution)/shard_map/all_gather | solution.py:65
  391.9 26.3 %fusion = f32[304,2048]{1,0:T(8,128)S(1)} fusion(bf16[8192,2048]{1,0:T(8,128)(2,1)} %all-gather.2.cloned.1.call-done, bf16[38,8,64,128]{3,2,1,0:T(8,128)(2,1)} %bitcast.16), kind=kOutput, calls=%fused_computation | convolution fusion | flops 10200547328 | bytes 41025536 | tf_op jit(solution)/shard_map/dot_general | solution.py:14
  418.3 0.0 copy-start.3
  418.3 0.0 copy-start.4
  418.3 0.0 copy-start.5
  418.3 0.0 copy-start.7
  418.3 0.0 copy-start.8
  418.3 0.0 copy-start.9
  418.3 4.2 multiply_reduce_fusion
  422.5 0.0 copy-done.4
  422.5 1.3 multiply_reduce_fusion.1
  423.9 0.9 multiply_reduce_fusion.2
  424.7 5.8 %all-reduce = (f32[64]{0:T(128)S(1)}, f32[16]{0:T(128)S(1)}, f32[224]{0:T(256)S(1)}) all-reduce(f32[64]{0:T(128)S(1)} %get-tuple-element.16, f32[16]{0:T(128)S(1)} %get-tuple-element.14, f32[224]{0:T(256)S(1)} %get-tuple-element.12), channel_id=1, replica_groups=mesh['col'=4,'dp'=64] {'col'}, use_global_device_ids=true, to_apply=%region_1.0 | all-reduce | flops 304 | bytes 2432 | tf_op jit(solution)/shard_map/psum | solution.py:77
  430.5 1.1 divide_convert_fusion
  431.7 0.7 divide_convert_fusion.2
  432.4 0.8 divide_convert_fusion.1
  (16 shorter events, 0.1 us)
Async XLA Ops:
  7.2 384.7 %all-gather.2.cloned.1.call-start = ((), (), s32[]{:S(2)}) async-start(), calls=%async_computation.1 | async-start | bytes 34078720 | tf_op jit(solution)/shard_map/all_gather | solution.py:65
  7.9 6.2 %copy-start = (bf16[128,4096]{1,0:T(8,128)(2,1)S(1)}, bf16[128,4096]{1,0:T(8,128)(2,1)}, u32[]{:S(2)}) copy-start(bf16[128,4096]{1,0:T(8,128)(2,1)} %param.14) | copy-start | bytes 3145732
  7.9 6.8 %copy-start.6 = (bf16[128,1024]{1,0:T(8,128)(2,1)S(1)}, bf16[128,1024]{1,0:T(8,128)(2,1)}, u32[]{:S(2)}) copy-start(bf16[128,1024]{1,0:T(8,128)(2,1)} %param.15) | copy-start | bytes 786436
  391.9 26.3 %copy-start.1 = (bf16[224,2048]{1,0:T(8,128)(2,1)S(1)}, bf16[224,2048]{1,0:T(8,128)(2,1)}, u32[]{:S(2)}) copy-start(bf16[224,2048]{1,0:T(8,128)(2,1)} %param.25) | copy-start | bytes 2752516
  391.9 26.3 %copy-start.2 = (bf16[224,2048]{1,0:T(8,128)(2,1)S(1)}, bf16[224,2048]{1,0:T(8,128)(2,1)}, u32[]{:S(2)}) copy-start(bf16[224,2048]{1,0:T(8,128)(2,1)} %param.22) | copy-start | bytes 2752516
  418.3 4.2 copy-start.3
  418.3 4.2 copy-start.4
  418.3 4.2 copy-start.5
  418.3 5.5 %copy-start.7 = (bf16[16,2048]{1,0:T(8,128)(2,1)S(1)}, bf16[16,2048]{1,0:T(8,128)(2,1)}, u32[]{:S(2)}) copy-start(bf16[16,2048]{1,0:T(8,128)(2,1)} %param.24) | copy-start | bytes 196612
  418.3 5.5 %copy-start.8 = (bf16[16,2048]{1,0:T(8,128)(2,1)S(1)}, bf16[16,2048]{1,0:T(8,128)(2,1)}, u32[]{:S(2)}) copy-start(bf16[16,2048]{1,0:T(8,128)(2,1)} %param.21) | copy-start | bytes 196612
  418.3 5.5 %copy-start.9 = (bf16[16,2048]{1,0:T(8,128)(2,1)S(1)}, bf16[16,2048]{1,0:T(8,128)(2,1)}, u32[]{:S(2)}) copy-start(bf16[16,2048]{1,0:T(8,128)(2,1)} %param.18) | copy-start | bytes 196612
Sparse Core Ops, SparseCore 0:
  11.3 380.5 all-gather.1
where the time goes:
time: 440 us
  waiting for transfers between devices  189 us (43%)
  blocking collectives  188 us (43%)
  matrix products  26.3 us (6%)
  between operations  14.2 us (3%)
  other arithmetic  11.3 us (3%)
  local copies, waits for them, and re-layouts  10.7 us (2%)
    all_gather x1, waiting for transfers between devices, per_device(): gathered = lax.all_gather(layer_input, 'dp', axis=0, tiled=True)  189 us
    all_to_all x1, blocking collectives, per_device(): lax.all_to_all(joined, 'dp', split_axis=1, concat_axis=0, tiled=True)  182 us
    dot_general x1, matrix products, contract_tokens(): lax.dot_general(cotangent_rows, inputs, (((0,), (0,)), ((), ())), preferr...  26.3 us
  transfers between devices with their start and end apart: 1, of which 1 were waited for; matrix products, arithmetic and copies ran while one was open for 3% of the time, Pallas kernels for 0%

commit v1 on v0

--- a/solution.py
+++ b/solution.py
@@ -62,7 +62,10 @@
     owned = lax.all_to_all(joined, "dp", split_axis=1, concat_axis=0, tiled=True).reshape(
         -1, all_rows
     )
-    gathered = lax.all_gather(layer_input, "dp", axis=0, tiled=True)
+    size = lax.axis_size("dp")
+    parts = jnp.stack([layer_input for _ in range(size)])
+    parts = lax.all_to_all(parts, "dp", split_axis=0, concat_axis=0)
+    gathered = jnp.concatenate(parts, axis=0)
     gradient = contract_tokens(owned, gathered)
     grad_query = gradient[:query_rows]
     grad_key = gradient[query_rows : query_rows + key_rows]

time: 440 us -> 1030 us (2.34)
  the two profiles are of different devices: /device:TPU:6 before, /device:TPU:162 now
where the time goes in v1:
time: 1030 us
  waiting for transfers between devices  823 us (80%)
  blocking collectives  129 us (13%)
  matrix products  26.2 us (3%)
  local copies, waits for them, and re-layouts  23.9 us (2%)
  other arithmetic  11.6 us (1%)
  starting transfers between devices  11.3 us (1%)
    all_to_all x1, waiting for transfers between devices, per_device(): parts = lax.all_to_all(parts, 'dp', split_axis=0, concat_axis=0)  823 us
    all_to_all x1, blocking collectives, per_device(): lax.all_to_all(joined, 'dp', split_axis=1, concat_axis=0, tiled=True)  123 us
    dot_general x1, matrix products, contract_tokens(): lax.dot_general(cotangent_rows, inputs, (((0,), (0,)), ((), ())), preferr...  26.2 us
  transfers between devices with their start and end apart: 1, of which 1 were waited for; matrix products, arithmetic and copies ran while one was open for 1% of the time, Pallas kernels for 0%

profile of v1, /device:TPU:162, one launch (start us, length us, event | category | flops | bytes accessed | tf_op | source)
XLA Modules:
  0.0 1025.9 jit_solution(17596896096685570473)
XLA Ops:
  0.7 6.1 copy.24
  6.8 0.7 copy.22
  7.5 0.2 copy.23
  7.6 2.2 pad_maximum_fusion
  9.9 0.0 copy-start.2
  9.9 123.2 %all_to_all.20 = bf16[128,64,304]{0,2,1:T(8,128)(2,1)} all-to-all(bf16[128,64,304]{0,2,1:T(8,128)(2,1)S(1)} %pad_maximum_fusion), channel_id=1, replica_groups=mesh['col'=4,'dp'=64] {'dp'}, dimensions={1} | all-to-all | bytes 9961472 | tf_op jit(solution)/shard_map/all_to_all | solution.py:62
  133.1 11.0 %stack.2 = bf16[64,128,2048]{2,1,0:T(8,128)(2,1)} broadcast(bf16[128,2048]{1,0:T(8,128)(2,1)S(1)} %copy-done.2), dimensions={1,2} | broadcast | bytes 34078720 | tf_op jit(solution)/shard_map/stack | solution.py:66
  144.1 11.3 %all-to-all-start.1 = ((bf16[64,128,2048]{2,1,0:T(8,128)(2,1)}), bf16[64,128,2048]{2,1,0:T(8,128)(2,1)}, u32[]{:S(2)}, u32[]{:S(2)}) async-start(bf16[64,128,2048]{2,1,0:T(8,128)(2,1)} %stack.2), calls=%async_computation.1 | async-start | bytes 67108864 | tf_op jit(solution)/shard_map/all_to_all | solution.py:67
  155.4 6.0 copy.25
  161.3 823.1 %all-to-all-done.1 = bf16[64,128,2048]{2,1,0:T(8,128)(2,1)} async-done(((bf16[64,128,2048]{2,1,0:T(8,128)(2,1)}), bf16[64,128,2048]{2,1,0:T(8,128)(2,1)}, u32[]{:S(2)}, u32[]{:S(2)}) %all-to-all-start.1) | async-done | bytes 33554464 | tf_op jit(solution)/shard_map/all_to_all | solution.py:67
  984.4 26.2 %fusion = f32[304,2048]{1,0:T(8,128)S(1)} fusion(bf16[8192,2048]{1,0:T(8,128)(2,1)} %bitcast.5, bf16[38,8,64,128]{3,2,1,0:T(8,128)(2,1)} %bitcast.17), kind=kOutput, calls=%fused_computation | convolution fusion | flops 10200547328 | bytes 41025536 | tf_op jit(solution)/shard_map/dot_general | solution.py:14
  1010.7 0.0 copy-start.3
  1010.7 0.0 copy-start.4
  1010.7 0.0 copy-start.5
  1010.7 0.0 copy-start.7
  1010.7 0.0 copy-start.8
  1010.7 0.0 copy-start.9
  1010.8 4.5 multiply_reduce_fusion
  1015.2 1.3 multiply_reduce_fusion.1
  1016.6 0.9 multiply_reduce_fusion.2
  1017.4 5.8 all-reduce
  1023.2 1.1 divide_convert_fusion
  1024.4 0.7 divide_convert_fusion.2
  1025.1 0.8 divide_convert_fusion.1
  (16 shorter events, 0.1 us)
Async XLA Ops:
  0.6 6.2 copy-start
  0.7 6.8 copy-start.6
  9.9 123.2 %copy-start.2 = (bf16[128,2048]{1,0:T(8,128)(2,1)S(1)}, bf16[128,2048]{1,0:T(8,128)(2,1)}, u32[]{:S(2)}) copy-start(bf16[128,2048]{1,0:T(8,128)(2,1)} %param.13) | copy-start | bytes 1572868
  144.1 840.3 %all-to-all-start.1 = ((bf16[64,128,2048]{2,1,0:T(8,128)(2,1)}), bf16[64,128,2048]{2,1,0:T(8,128)(2,1)}, u32[]{:S(2)}, u32[]{:S(2)}) async-start(bf16[64,128,2048]{2,1,0:T(8,128)(2,1)} %stack.2), calls=%async_computation.1 | async-start | bytes 67108864 | tf_op jit(solution)/shard_map/all_to_all | solution.py:67
  984.4 26.3 %copy-start.1 = (bf16[224,2048]{1,0:T(8,128)(2,1)S(1)}, bf16[224,2048]{1,0:T(8,128)(2,1)}, u32[]{:S(2)}) copy-start(bf16[224,2048]{1,0:T(8,128)(2,1)} %param.25) | copy-start | bytes 2752516
  1010.7 4.5 copy-start.3
  1010.7 4.5 copy-start.4
  1010.7 4.5 copy-start.5
  1010.7 5.8 copy-start.7
  1010.7 5.8 copy-start.8
  1010.7 5.8 copy-start.9
